TPU v7x, 32 devices: a whole 2x2x4 slice. The times are simulated.
32 devices in a mesh: rep: 2 (over x), grp: 4 (over z), tp: 4 (over y, core).
Axes of the slice: x: 2, y: 2, z: 4, core: 2. Of those that a mesh axis runs over, the one named last changes fastest.
Arguments:
- queries: bfloat16 [512, 8192], P(('rep', 'grp'), 'tp'), parts along dimension 0, may hold values from -256 to 256
- newest_key_value: bfloat16 [512, 2, 1024], P(('rep', 'grp')), parts along dimension 0, may hold values from -6 to 6
- kv_pages: bfloat16 [128, 2, 128, 1024], P(('rep', 'grp', 'tp')), parts along dimension 0, may hold values from -8 to 8
- fetch_slots: int32 [8, 16, 2], P('rep', ('grp', 'tp')), parts along dimension 0, may hold values from -1 to 3, as said below
- block_table: int32 [512, 8], P(('rep', 'grp')), parts along dimension 0, may hold values from 0 to 31, as said below
- prefix_len: int32 [512], P(('rep', 'grp')), parts along dimension 0, may hold values from 2 to 1024
- out_weight: bfloat16 [8192, 8192], P('tp'), may hold values from -0.09375 to 0.09375
Outputs:
- attended: bfloat16 [512, 8192], P(('rep', 'grp'), 'tp'), parts along dimension 0
There are 2 independent parts, one for each index of `rep`. A program takes and returns all parts, laid end to end along the dimension named above; an argument that names none is the same for every part. Nothing has to cross between parts.
Inputs may be any that keep to these rules, and one draw needn't show every extreme that they name: `fetch_slots`: entries of one (group, owner device) are distinct pages of that device's storage; each group takes at most 2 pages from one device, and in every draw some group takes exactly 2 from some device; -1 marks an unused entry, and used entries come first. `block_table`: every entry names a used entry of its group's fetch_slots; requests of a group share their first pages to a varying depth.
All inputs are finite; a program needn't handle non-finite values.
Results may differ from a plain program's by a relative error of at most 0.0057.
Values may be sent and summed in bfloat16 or wider, within the bound.
A program may use at most 128 MiB of HBM per device.

v0:
```python
import math

import jax
import jax.numpy as jnp
from jax import lax
from jax.sharding import PartitionSpec as P

QUERY_HEADS = 64
KEY_VALUE_HEADS = 8
HEAD_SIZE = 128
PAGE_TOKENS = 128
PAGE_LIST_LENGTH = 8
GROUP_PAGE_LIMIT = 2


def per_device(
    queries, newest_key_value, kv_pages, fetch_slots, block_table, prefix_len, out_weight
):
    tp_count = lax.axis_size("tp")
    group_count = lax.axis_size("grp")
    tp_rank = lax.axis_index("tp")
    group_width = QUERY_HEADS // KEY_VALUE_HEADS
    heads_dev = queries.shape[1] // HEAD_SIZE
    kv_dev = max(1, heads_dev // group_width)
    per_kv = heads_dev // kv_dev
    kv_width = kv_dev * HEAD_SIZE
    kv_first = tp_rank * heads_dev // group_width
    req_rows = queries.shape[0]
    targets = jnp.arange(tp_count)
    head_index = (targets * heads_dev // group_width)[:, None] + jnp.arange(kv_dev)[None, :]
    wanted = jnp.maximum(fetch_slots.reshape(group_count * GROUP_PAGE_LIMIT), 0)
    chosen_pages = jnp.take(kv_pages, wanted, axis=0)
    chosen_pages = chosen_pages.reshape(
        group_count, GROUP_PAGE_LIMIT, 2, PAGE_TOKENS, KEY_VALUE_HEADS, HEAD_SIZE
    )
    pieces = jnp.take(chosen_pages, head_index.reshape(-1), axis=4)
    pieces = pieces.reshape(group_count, GROUP_PAGE_LIMIT, 2, PAGE_TOKENS, tp_count, kv_width)
    outgoing = jnp.transpose(pieces, (0, 4, 1, 2, 3, 5)).reshape(
        group_count * tp_count * GROUP_PAGE_LIMIT, 2, PAGE_TOKENS, kv_width
    )
    fetched = lax.all_to_all(outgoing, ("grp", "tp"), split_axis=0, concat_axis=0, tiled=True)
    newest_token = lax.dynamic_slice_in_dim(
        newest_key_value, kv_first * HEAD_SIZE, kv_width, 2
    ).reshape(req_rows, 2, kv_dev, HEAD_SIZE)
    block_rows = math.gcd(req_rows, 8)
    steps_count = req_rows // block_rows
    query_blocks = queries.reshape(steps_count, block_rows, kv_dev, per_kv, HEAD_SIZE)
    fresh_blocks = newest_token.reshape(steps_count, block_rows, 2, kv_dev, HEAD_SIZE)
    table_blocks = block_table.reshape(steps_count, block_rows, PAGE_LIST_LENGTH)
    length_blocks = prefix_len.reshape(steps_count, block_rows)
    score_scale = 1.0 / math.sqrt(HEAD_SIZE)
    positions = jnp.arange(PAGE_LIST_LENGTH * PAGE_TOKENS)

    def attend(inputs):
        query_tile, newest_block, table_block, length_block = inputs
        gathered = fetched[table_block]
        key_matrix = gathered[:, :, 0].reshape(
            block_rows, PAGE_LIST_LENGTH * PAGE_TOKENS, kv_dev, HEAD_SIZE
        )
        value_matrix = gathered[:, :, 1].reshape(
            block_rows, PAGE_LIST_LENGTH * PAGE_TOKENS, kv_dev, HEAD_SIZE
        )
        scores = (
            jnp.einsum(
                "bkqd,bpkd->bkqp", query_tile, key_matrix, preferred_element_type=jnp.float32
            )
            * score_scale
        )
        live_mask = positions[None, :] < length_block[:, None]
        scores = jnp.where(live_mask[:, None, None, :], scores, -jnp.inf)
        own_score = (
            jnp.einsum(
                "xzcu,xzu->xzc", query_tile, newest_block[:, 0], preferred_element_type=jnp.float32
            )
            * score_scale
        )
        row_top = jnp.maximum(jnp.max(scores, axis=-1), own_score)
        exp_terms = jnp.exp(scores - row_top[..., None])
        exp_own = jnp.exp(own_score - row_top)
        denom_sum = jnp.sum(exp_terms, axis=-1) + exp_own
        weights = (exp_terms / denom_sum[..., None]).astype(jnp.bfloat16)
        weight_own = (exp_own / denom_sum).astype(jnp.bfloat16).astype(jnp.float32)
        mixed = jnp.einsum(
            "bkqp,bpkd->bkqd", weights, value_matrix, preferred_element_type=jnp.float32
        )
        mixed = (
            mixed + weight_own[..., None] * newest_block[:, 1].astype(jnp.float32)[:, :, None, :]
        )
        return mixed.astype(jnp.bfloat16).reshape(block_rows, heads_dev * HEAD_SIZE)

    mix = lax.map(attend, (query_blocks, fresh_blocks, table_blocks, length_blocks)).reshape(
        req_rows, heads_dev * HEAD_SIZE
    )
    partial_out = jnp.dot(mix, out_weight, preferred_element_type=jnp.float32)
    summed = lax.psum_scatter(partial_out, "tp", scatter_dimension=1, tiled=True)
    return summed.astype(jnp.bfloat16)


def solution(mesh):
    in_specs = (
        P(("rep", "grp"), "tp"),
        P(("rep", "grp"), None, None),
        P(("rep", "grp", "tp"), None, None, None),
        P("rep", ("grp", "tp"), None),
        P(("rep", "grp"), None),
        P(("rep", "grp")),
        P("tp", None),
    )
    out_specs = P(("rep", "grp"), "tp")
    return jax.shard_map(
        per_device, mesh=mesh, in_specs=in_specs, out_specs=out_specs, check_vma=False
    )
```

profile of v0, /device:TPU:1, one launch (start us, length us, event | category | flops | bytes accessed | tf_op | source)
XLA Modules:
  0.0 483.2 jit_solution(15578746208180226145)
XLA Ops:
  6.5 0.8 broadcast_maximum_fusion
  8.5 2.8 gather_fusion.1
  11.3 6.4 %copy.43 = bf16[8,2,128,1024]{2,3,1,0:T(8,128)(2,1)} copy(bf16[8,2,128,1024]{3,2,1,0:T(8,128)(2,1)} %gather_fusion.1) | data formatting | bytes 8388608 | tf_op jit(solution)/shard_map/jit(_take)/gather | solution.py:32
  17.7 6.3 %copy.44 = bf16[4,2,2,128,8,128]{5,3,4,2,1,0:T(8,128)(2,1)} copy(bf16[4,2,2,128,8,128]{3,5,4,2,1,0:T(8,128)(2,1)} %bitcast.79) | data formatting | bytes 8388608 | tf_op jit(solution)/shard_map/jit(_take)/gather | solution.py:32
  24.1 4.6 broadcast_select_fusion
  28.7 5.2 %gather_fusion.2 = bf16[8,4,2,2,128,128]{5,4,3,2,1,0:T(8,128)(2,1)} fusion(bf16[4,2,2,128,8,128]{5,3,4,2,1,0:T(8,128)(2,1)} %broadcast_select_fusion, s32[1024]{0:T(1024)S(1)} %pad_clamp_fusion.1), kind=kCustom, calls=%fused_computation.2 | custom fusion | bytes 8388640 | tf_op jit(solution)/shard_map/jit(_take)/gather | solution.py:36
  33.9 6.3 %copy.45 = bf16[4,2,2,128,8,128]{3,5,4,2,1,0:T(8,128)(2,1)} copy(bf16[4,2,2,128,8,128]{5,3,2,1,0,4:T(8,128)(2,1)} %bitcast.78) | data formatting | bytes 8388608 | tf_op jit(solution)/shard_map/jit(_take)/gather | solution.py:36
  40.4 4.7 fusion.33
  45.2 7.3 %copy.46 = bf16[4,4,2,2,128,256]{5,4,3,2,1,0:T(8,128)(2,1)} copy(bf16[4,4,2,2,128,256]{4,5,1,3,2,0:T(8,128)(2,1)} %fusion.33) | data formatting | bytes 8388608 | tf_op jit(solution)/shard_map/transpose | solution.py:38
  52.5 7.5 %all-to-all-start = ((bf16[32,2,128,256]{3,2,1,0:T(8,128)(2,1)}), bf16[32,2,128,256]{3,2,1,0:T(8,128)(2,1)}, u32[]{:S(2)}, u32[]{:S(2)}) async-start(bf16[32,2,128,256]{3,2,1,0:T(8,128)(2,1)} %bitcast.76), calls=%async_computation | async-start | bytes 8388608 | tf_op jit(solution)/shard_map/all_to_all | solution.py:41
  60.0 0.9 constant_dynamic-slice_fusion.2
  61.2 76.9 %all-to-all-done = bf16[32,2,128,256]{3,2,1,0:T(8,128)(2,1)} async-done(((bf16[32,2,128,256]{3,2,1,0:T(8,128)(2,1)}), bf16[32,2,128,256]{3,2,1,0:T(8,128)(2,1)}, u32[]{:S(2)}, u32[]{:S(2)}) %all-to-all-start) | async-done | bytes 4194336 | tf_op jit(solution)/shard_map/all_to_all | solution.py:41
  138.1 276.4 %while.11 = (s32[]{:T(128)}, bf16[8,8,2048]{2,1,0:T(8,128)(2,1)S(1)}, s32[8,8]{1,0:T(8,128)S(1)}, bf16[8,8,2,8,128]{4,3,2,1,0:T(8,128)(2,1)S(1)}, s32[8,8,8]{2,1...) while((s32[]{:T(128)}, ...), condition=%wide.region_3.4_spmd.clone, body=%wide.region_0.3_spmd.clone.sunk | while | flops 68251712 | bytes 60601548 | solution.py:91
  138.2 7.6 %gather_fusion = bf16[64,2,128,256]{3,2,1,0:T(8,128)(2,1)} fusion(bf16[32,2,128,256]{3,2,1,0:T(8,128)(2,1)} %get-tuple-element.187, s32[1024]{0:T(1024)S(1)} %pad_clamp_fusion.4), kind=kCustom, calls=%fused_computation.clone.clone.1 | custom fusion | bytes 16777472 | tf_op jit(solution)/shard_map/while/body/eval_jaxpr/gather | solution.py:56
  145.8 6.0 %fusion.54 = (bf16[8,8,1,128,256]{4,3,2,1,0:T(8,128)(2,1)}, bf16[8,8,1,128,256]{4,3,2,1,0:T(8,128)(2,1)}) fusion(bf16[8,8,2,128,256]{4,3,2,1,0:T(8,128)(2,1)} %bitcast.75), kind=kLoop, calls=%fused_computation.62.clone.1 | loop fusion | bytes 16777216 | tf_op jit(solution)/shard_map/while/body/eval_jaxpr/slice | solution.py:57
  151.8 6.9 %reshape.222 = bf16[8,1024,2,128]{3,2,1,0:T(2,128)(2,1)} reshape(bf16[8,8,1,128,256]{4,3,2,1,0:T(8,128)(2,1)} %get-tuple-element.159) | data formatting | bytes 8388608 | tf_op jit(solution)/shard_map/while/body/eval_jaxpr/reshape;while/body/eval_jaxpr/squeeze | solution.py:57
  158.8 3.5 fusion.56
  162.7 6.9 %reshape.221 = bf16[8,1024,2,128]{3,2,1,0:T(2,128)(2,1)} reshape(bf16[8,8,1,128,256]{4,3,2,1,0:T(8,128)(2,1)} %get-tuple-element.158) | data formatting | bytes 8388608 | tf_op jit(solution)/shard_map/while/body/eval_jaxpr/reshape;while/body/eval_jaxpr/squeeze | solution.py:60
  169.6 3.0 fusion.61
  172.7 7.6 %gather_fusion = bf16[64,2,128,256]{3,2,1,0:T(8,128)(2,1)} fusion(bf16[32,2,128,256]{3,2,1,0:T(8,128)(2,1)} %get-tuple-element.187, s32[1024]{0:T(1024)S(1)} %pad_clamp_fusion.4), kind=kCustom, calls=%fused_computation.clone.clone.1 | custom fusion | bytes 16777472 | tf_op jit(solution)/shard_map/while/body/eval_jaxpr/gather | solution.py:56
  180.4 6.0 %fusion.54 = (bf16[8,8,1,128,256]{4,3,2,1,0:T(8,128)(2,1)}, bf16[8,8,1,128,256]{4,3,2,1,0:T(8,128)(2,1)}) fusion(bf16[8,8,2,128,256]{4,3,2,1,0:T(8,128)(2,1)} %bitcast.75), kind=kLoop, calls=%fused_computation.62.clone.1 | loop fusion | bytes 16777216 | tf_op jit(solution)/shard_map/while/body/eval_jaxpr/slice | solution.py:57
  186.4 6.9 %reshape.222 = bf16[8,1024,2,128]{3,2,1,0:T(2,128)(2,1)} reshape(bf16[8,8,1,128,256]{4,3,2,1,0:T(8,128)(2,1)} %get-tuple-element.159) | data formatting | bytes 8388608 | tf_op jit(solution)/shard_map/while/body/eval_jaxpr/reshape;while/body/eval_jaxpr/squeeze | solution.py:57
  193.3 3.5 fusion.56
  197.3 6.9 %reshape.221 = bf16[8,1024,2,128]{3,2,1,0:T(2,128)(2,1)} reshape(bf16[8,8,1,128,256]{4,3,2,1,0:T(8,128)(2,1)} %get-tuple-element.158) | data formatting | bytes 8388608 | tf_op jit(solution)/shard_map/while/body/eval_jaxpr/reshape;while/body/eval_jaxpr/squeeze | solution.py:60
  204.2 3.0 fusion.61
  207.3 7.6 %gather_fusion = bf16[64,2,128,256]{3,2,1,0:T(8,128)(2,1)} fusion(bf16[32,2,128,256]{3,2,1,0:T(8,128)(2,1)} %get-tuple-element.187, s32[1024]{0:T(1024)S(1)} %pad_clamp_fusion.4), kind=kCustom, calls=%fused_computation.clone.clone.1 | custom fusion | bytes 16777472 | tf_op jit(solution)/shard_map/while/body/eval_jaxpr/gather | solution.py:56
  214.9 6.0 %fusion.54 = (bf16[8,8,1,128,256]{4,3,2,1,0:T(8,128)(2,1)}, bf16[8,8,1,128,256]{4,3,2,1,0:T(8,128)(2,1)}) fusion(bf16[8,8,2,128,256]{4,3,2,1,0:T(8,128)(2,1)} %bitcast.75), kind=kLoop, calls=%fused_computation.62.clone.1 | loop fusion | bytes 16777216 | tf_op jit(solution)/shard_map/while/body/eval_jaxpr/slice | solution.py:57
  220.9 6.9 %reshape.222 = bf16[8,1024,2,128]{3,2,1,0:T(2,128)(2,1)} reshape(bf16[8,8,1,128,256]{4,3,2,1,0:T(8,128)(2,1)} %get-tuple-element.159) | data formatting | bytes 8388608 | tf_op jit(solution)/shard_map/while/body/eval_jaxpr/reshape;while/body/eval_jaxpr/squeeze | solution.py:57
  227.9 3.5 fusion.56
  231.8 6.9 %reshape.221 = bf16[8,1024,2,128]{3,2,1,0:T(2,128)(2,1)} reshape(bf16[8,8,1,128,256]{4,3,2,1,0:T(8,128)(2,1)} %get-tuple-element.158) | data formatting | bytes 8388608 | tf_op jit(solution)/shard_map/while/body/eval_jaxpr/reshape;while/body/eval_jaxpr/squeeze | solution.py:60
  238.7 3.0 fusion.61
  241.9 7.7 %gather_fusion = bf16[64,2,128,256]{3,2,1,0:T(8,128)(2,1)} fusion(bf16[32,2,128,256]{3,2,1,0:T(8,128)(2,1)} %get-tuple-element.187, s32[1024]{0:T(1024)S(1)} %pad_clamp_fusion.4), kind=kCustom, calls=%fused_computation.clone.clone.1 | custom fusion | bytes 16777472 | tf_op jit(solution)/shard_map/while/body/eval_jaxpr/gather | solution.py:56
  249.5 6.0 %fusion.54 = (bf16[8,8,1,128,256]{4,3,2,1,0:T(8,128)(2,1)}, bf16[8,8,1,128,256]{4,3,2,1,0:T(8,128)(2,1)}) fusion(bf16[8,8,2,128,256]{4,3,2,1,0:T(8,128)(2,1)} %bitcast.75), kind=kLoop, calls=%fused_computation.62.clone.1 | loop fusion | bytes 16777216 | tf_op jit(solution)/shard_map/while/body/eval_jaxpr/slice | solution.py:57
  255.5 6.9 %reshape.222 = bf16[8,1024,2,128]{3,2,1,0:T(2,128)(2,1)} reshape(bf16[8,8,1,128,256]{4,3,2,1,0:T(8,128)(2,1)} %get-tuple-element.159) | data formatting | bytes 8388608 | tf_op jit(solution)/shard_map/while/body/eval_jaxpr/reshape;while/body/eval_jaxpr/squeeze | solution.py:57
  262.5 3.5 fusion.56
  266.4 6.9 %reshape.221 = bf16[8,1024,2,128]{3,2,1,0:T(2,128)(2,1)} reshape(bf16[8,8,1,128,256]{4,3,2,1,0:T(8,128)(2,1)} %get-tuple-element.158) | data formatting | bytes 8388608 | tf_op jit(solution)/shard_map/while/body/eval_jaxpr/reshape;while/body/eval_jaxpr/squeeze | solution.py:60
  273.3 3.0 fusion.61
  276.4 7.6 %gather_fusion = bf16[64,2,128,256]{3,2,1,0:T(8,128)(2,1)} fusion(bf16[32,2,128,256]{3,2,1,0:T(8,128)(2,1)} %get-tuple-element.187, s32[1024]{0:T(1024)S(1)} %pad_clamp_fusion.4), kind=kCustom, calls=%fused_computation.clone.clone.1 | custom fusion | bytes 16777472 | tf_op jit(solution)/shard_map/while/body/eval_jaxpr/gather | solution.py:56
  284.1 6.0 %fusion.54 = (bf16[8,8,1,128,256]{4,3,2,1,0:T(8,128)(2,1)}, bf16[8,8,1,128,256]{4,3,2,1,0:T(8,128)(2,1)}) fusion(bf16[8,8,2,128,256]{4,3,2,1,0:T(8,128)(2,1)} %bitcast.75), kind=kLoop, calls=%fused_computation.62.clone.1 | loop fusion | bytes 16777216 | tf_op jit(solution)/shard_map/while/body/eval_jaxpr/slice | solution.py:57
  290.1 6.9 %reshape.222 = bf16[8,1024,2,128]{3,2,1,0:T(2,128)(2,1)} reshape(bf16[8,8,1,128,256]{4,3,2,1,0:T(8,128)(2,1)} %get-tuple-element.159) | data formatting | bytes 8388608 | tf_op jit(solution)/shard_map/while/body/eval_jaxpr/reshape;while/body/eval_jaxpr/squeeze | solution.py:57
  297.0 3.5 fusion.56
  301.0 6.9 %reshape.221 = bf16[8,1024,2,128]{3,2,1,0:T(2,128)(2,1)} reshape(bf16[8,8,1,128,256]{4,3,2,1,0:T(8,128)(2,1)} %get-tuple-element.158) | data formatting | bytes 8388608 | tf_op jit(solution)/shard_map/while/body/eval_jaxpr/reshape;while/body/eval_jaxpr/squeeze | solution.py:60
  307.9 3.0 fusion.61
  311.0 7.6 %gather_fusion = bf16[64,2,128,256]{3,2,1,0:T(8,128)(2,1)} fusion(bf16[32,2,128,256]{3,2,1,0:T(8,128)(2,1)} %get-tuple-element.187, s32[1024]{0:T(1024)S(1)} %pad_clamp_fusion.4), kind=kCustom, calls=%fused_computation.clone.clone.1 | custom fusion | bytes 16777472 | tf_op jit(solution)/shard_map/while/body/eval_jaxpr/gather | solution.py:56
  318.6 6.0 %fusion.54 = (bf16[8,8,1,128,256]{4,3,2,1,0:T(8,128)(2,1)}, bf16[8,8,1,128,256]{4,3,2,1,0:T(8,128)(2,1)}) fusion(bf16[8,8,2,128,256]{4,3,2,1,0:T(8,128)(2,1)} %bitcast.75), kind=kLoop, calls=%fused_computation.62.clone.1 | loop fusion | bytes 16777216 | tf_op jit(solution)/shard_map/while/body/eval_jaxpr/slice | solution.py:57
  324.6 6.9 %reshape.222 = bf16[8,1024,2,128]{3,2,1,0:T(2,128)(2,1)} reshape(bf16[8,8,1,128,256]{4,3,2,1,0:T(8,128)(2,1)} %get-tuple-element.159) | data formatting | bytes 8388608 | tf_op jit(solution)/shard_map/while/body/eval_jaxpr/reshape;while/body/eval_jaxpr/squeeze | solution.py:57
  331.5 3.5 fusion.56
  335.5 6.9 %reshape.221 = bf16[8,1024,2,128]{3,2,1,0:T(2,128)(2,1)} reshape(bf16[8,8,1,128,256]{4,3,2,1,0:T(8,128)(2,1)} %get-tuple-element.158) | data formatting | bytes 8388608 | tf_op jit(solution)/shard_map/while/body/eval_jaxpr/reshape;while/body/eval_jaxpr/squeeze | solution.py:60
  342.4 3.0 fusion.61
  345.5 7.7 %gather_fusion = bf16[64,2,128,256]{3,2,1,0:T(8,128)(2,1)} fusion(bf16[32,2,128,256]{3,2,1,0:T(8,128)(2,1)} %get-tuple-element.187, s32[1024]{0:T(1024)S(1)} %pad_clamp_fusion.4), kind=kCustom, calls=%fused_computation.clone.clone.1 | custom fusion | bytes 16777472 | tf_op jit(solution)/shard_map/while/body/eval_jaxpr/gather | solution.py:56
  353.2 6.0 %fusion.54 = (bf16[8,8,1,128,256]{4,3,2,1,0:T(8,128)(2,1)}, bf16[8,8,1,128,256]{4,3,2,1,0:T(8,128)(2,1)}) fusion(bf16[8,8,2,128,256]{4,3,2,1,0:T(8,128)(2,1)} %bitcast.75), kind=kLoop, calls=%fused_computation.62.clone.1 | loop fusion | bytes 16777216 | tf_op jit(solution)/shard_map/while/body/eval_jaxpr/slice | solution.py:57
  359.1 6.9 %reshape.222 = bf16[8,1024,2,128]{3,2,1,0:T(2,128)(2,1)} reshape(bf16[8,8,1,128,256]{4,3,2,1,0:T(8,128)(2,1)} %get-tuple-element.159) | data formatting | bytes 8388608 | tf_op jit(solution)/shard_map/while/body/eval_jaxpr/reshape;while/body/eval_jaxpr/squeeze | solution.py:57
  366.1 3.5 fusion.56
  370.1 6.9 %reshape.221 = bf16[8,1024,2,128]{3,2,1,0:T(2,128)(2,1)} reshape(bf16[8,8,1,128,256]{4,3,2,1,0:T(8,128)(2,1)} %get-tuple-element.158) | data formatting | bytes 8388608 | tf_op jit(solution)/shard_map/while/body/eval_jaxpr/reshape;while/body/eval_jaxpr/squeeze | solution.py:60
  377.0 3.0 fusion.61
  380.1 7.6 %gather_fusion = bf16[64,2,128,256]{3,2,1,0:T(8,128)(2,1)} fusion(bf16[32,2,128,256]{3,2,1,0:T(8,128)(2,1)} %get-tuple-element.187, s32[1024]{0:T(1024)S(1)} %pad_clamp_fusion.4), kind=kCustom, calls=%fused_computation.clone.clone.1 | custom fusion | bytes 16777472 | tf_op jit(solution)/shard_map/while/body/eval_jaxpr/gather | solution.py:56
  387.7 6.0 %fusion.54 = (bf16[8,8,1,128,256]{4,3,2,1,0:T(8,128)(2,1)}, bf16[8,8,1,128,256]{4,3,2,1,0:T(8,128)(2,1)}) fusion(bf16[8,8,2,128,256]{4,3,2,1,0:T(8,128)(2,1)} %bitcast.75), kind=kLoop, calls=%fused_computation.62.clone.1 | loop fusion | bytes 16777216 | tf_op jit(solution)/shard_map/while/body/eval_jaxpr/slice | solution.py:57
  393.7 6.9 %reshape.222 = bf16[8,1024,2,128]{3,2,1,0:T(2,128)(2,1)} reshape(bf16[8,8,1,128,256]{4,3,2,1,0:T(8,128)(2,1)} %get-tuple-element.159) | data formatting | bytes 8388608 | tf_op jit(solution)/shard_map/while/body/eval_jaxpr/reshape;while/body/eval_jaxpr/squeeze | solution.py:57
  400.7 3.5 fusion.56
  404.6 6.9 %reshape.221 = bf16[8,1024,2,128]{3,2,1,0:T(2,128)(2,1)} reshape(bf16[8,8,1,128,256]{4,3,2,1,0:T(8,128)(2,1)} %get-tuple-element.158) | data formatting | bytes 8388608 | tf_op jit(solution)/shard_map/while/body/eval_jaxpr/reshape;while/body/eval_jaxpr/squeeze | solution.py:60
  411.5 3.0 fusion.61
  414.6 15.1 %fusion.34 = f32[64,8192]{1,0:T(8,128)} fusion(bf16[2048,8192]{1,0:T(8,128)(2,1)} %param.15, bf16[8,8,2048]{2,1,0:T(8,128)(2,1)S(1)} %get-tuple-element.47), kind=kOutput, calls=%fused_computation.45 | convolution fusion | flops 2147483648 | bytes 35913728 | tf_op jit(solution)/shard_map/dot_general | solution.py:94
  429.7 44.9 %reduce-scatter.2.cloned.1.call-done = f32[64,2048]{1,0:T(8,128)} async-done(((f32[64,8192]{1,0:T(8,128)}), f32[64,2048]{1,0:T(8,128)}) %reduce-scatter.2.cloned.1.call-update) | async-done | bytes 524304 | tf_op jit(solution)/shard_map/reduce_scatter | solution.py:95
  474.5 1.8 convert_element_type.25
  (134 shorter events, 6.9 us)
Async XLA Ops:
  6.5 2.0 copy-start
  52.5 8.5 %copy-start.2 = (bf16[64,2048]{1,0:T(8,128)(2,1)S(1)}, bf16[64,2048]{1,0:T(8,128)(2,1)}, u32[]{:S(2)}) copy-start(bf16[64,2048]{1,0:T(8,128)(2,1)} %param.9) | copy-start | bytes 786436
  52.5 8.6 %copy-start.3 = (s32[64,8]{0,1:T(8,128)S(1)}, s32[64,8]{0,1:T(8,128)}, u32[]{:S(2)}) copy-start(s32[64,8]{0,1:T(8,128)} %param.13) | copy-start | bytes 6148
  52.5 8.7 %copy-start.4 = (s32[64]{0:T(128)S(1)}, s32[64]{0:T(128)}, u32[]{:S(2)}) copy-start(s32[64]{0:T(128)} %param.14) | copy-start | bytes 772
  52.5 85.6 %all-to-all-start = ((bf16[32,2,128,256]{3,2,1,0:T(8,128)(2,1)}), bf16[32,2,128,256]{3,2,1,0:T(8,128)(2,1)}, u32[]{:S(2)}, u32[]{:S(2)}) async-start(bf16[32,2,128,256]{3,2,1,0:T(8,128)(2,1)} %bitcast.76), calls=%async_computation | async-start | bytes 8388608 | tf_op jit(solution)/shard_map/all_to_all | solution.py:41
  60.0 414.6 %reduce-scatter.2.cloned.1.call-start = ((), (), s32[]{:S(2)}) async-start(), calls=%async_computation.2 | async-start | bytes 2621440 | tf_op jit(solution)/shard_map/reduce_scatter | solution.py:95
  414.5 61.8 %copy-start.1 = (bf16[4,2,128,1024]{3,2,1,0:T(8,128)(2,1)S(1)}, bf16[4,2,128,1024]{3,2,1,0:T(8,128)(2,1)}, u32[]{:S(2)}) copy-start(bf16[4,2,128,1024]{3,2,1,0:T(8,128)(2,1)} %param.11) | copy-start | bytes 6291460
Sparse Core Ops, SparseCore 0:
  429.8 44.7 reduce-scatter.1
where the time goes:
time: 488 us; the launch traced here: 483 us
  local copies, waits for them, and re-layouts  256 us (52%)
  waiting for transfers between devices  122 us (25%)
  matrix products  67.7 us (14%)
  other arithmetic  15.8 us (3%)
  between operations  13.5 us (3%)
  starting transfers between devices  7.51 us (2%)
    all_to_all x1, waiting for transfers between devices, per_device(): lax.all_to_all(outgoing, ('grp', 'tp'), split_axis=0, concat_axis=0, tile...  76.9 us
    gather x8, local copies, waits for them, and re-layouts, attend(): gathered = fetched[table_block]  61 us
    squeeze x8, local copies, waits for them, and re-layouts, attend(): gathered[:, :, 1]  55.2 us
    squeeze x8, local copies, waits for them, and re-layouts, attend(): gathered[:, :, 0]  55.2 us
    slice x8, local copies, waits for them, and re-layouts, attend(): gathered[:, :, 0]  47.7 us
    reduce_scatter x1, waiting for transfers between devices, per_device(): lax.psum_scatter(partial_out, 'tp', scatter_dimension=1, tiled=True)  44.9 us
    dot_general x8, matrix products, attend(): jnp.einsum('bkqd,bpkd->bkqp', query_tile, key_matrix, preferred_element_t...  27.8 us
    dot_general x8, matrix products, attend(): jnp.einsum('bkqp,bpkd->bkqd', weights, value_matrix, preferred_element_ty...  23.7 us
  transfers between devices with their start and end apart: 2, of which 2 were waited for; matrix products, arithmetic and copies ran while one was open for 0% of the time, Pallas kernels for 0%

commit v1 on v0

v1 whole, which is shorter than its diff:
```python
import functools
import math

import jax
import jax.numpy as jnp
from jax import lax
from jax.experimental import pallas as pl
from jax.experimental.pallas import tpu as pltpu
from jax.sharding import PartitionSpec as P

QUERY_HEADS = 64
KEY_VALUE_HEADS = 8
HEAD_SIZE = 128
GROUP_WIDTH = QUERY_HEADS // KEY_VALUE_HEADS
DEAD = -1e30
SCALE = math.log2(math.e) / math.sqrt(HEAD_SIZE)
MESH = pl.DeviceIdType.MESH
VMEM_LIMIT = 60 * 1024 * 1024

VMEM_SPEC = pl.BlockSpec(memory_space=pltpu.VMEM)
ANY_SPEC = pl.BlockSpec(memory_space=pl.ANY)


def meet(axes):
    barrier = pltpu.get_barrier_semaphore()
    total = 0
    for axis in axes:
        count = lax.axis_size(axis)
        me = lax.axis_index(axis)
        for d in range(1, count):
            pl.semaphore_signal(
                barrier, inc=1, device_id={axis: lax.rem(me + d, count)}, device_id_type=MESH
            )
        total += count - 1
    pl.semaphore_wait(barrier, total)


def spread(axis, source_of, dest_of, send_sem, recv_sem, own_sem):
    count = lax.axis_size(axis)
    me = lax.axis_index(axis)
    copies = []
    for d in range(1, count):
        target = lax.rem(me + d, count)
        copy = pltpu.make_async_remote_copy(
            src_ref=source_of(target),
            dst_ref=dest_of(me),
            send_sem=send_sem.at[d],
            recv_sem=recv_sem.at[d],
            device_id={axis: target},
            device_id_type=MESH,
        )
        copy.start()
        copies.append(copy)
    own = pltpu.make_async_copy(source_of(me), dest_of(me), own_sem)
    own.start()
    copies.append(own)
    return copies


def fetch_kernel(
    heads_dev, width, q_ref, kv_ref, meta_ref, em_ref,
    q_all, pages_all, meta_all, em_all,
    sems_a, sems_b, sems_c, sems_d, sems_e, sems_f, sems_g, sems_h, own_sems,
):
    meet(("tp", "grp"))

    def columns(t):
        first = (t * heads_dev // GROUP_WIDTH) * HEAD_SIZE
        return kv_ref.at[:, :, :, pl.ds(pl.multiple_of(first, HEAD_SIZE), width)]

    copies = spread("tp", columns, lambda t: pages_all.at[t], sems_a, sems_b, own_sems.at[0])
    copies += spread("grp", lambda g: q_ref, lambda g: q_all.at[g], sems_c, sems_d, own_sems.at[1])
    copies += spread("grp", lambda g: meta_ref, lambda g: meta_all.at[g], sems_e, sems_f, own_sems.at[2])
    copies += spread("tp", lambda t: em_ref, lambda t: em_all.at[t], sems_g, sems_h, own_sems.at[3])
    for copy in copies:
        copy.wait()


def attend_kernel(list_len, q_ref, pages_ref, meta_ref, em_ref, o_ref, st_ref, mask_ref):
    groups, rows, cols = q_ref.shape
    owners, per_owner, _, page, width = pages_ref.shape
    heads = cols // HEAD_SIZE
    kv_heads = width // HEAD_SIZE
    per_kv = heads // kv_heads
    tokens = owners * per_owner * page
    lane_j = lax.broadcasted_iota(jnp.int32, (rows, list_len), 1)
    lane_t = lax.broadcasted_iota(jnp.int32, (rows, page), 1)

    def build(step, carry):
        g, t = step // owners, step % owners
        meta = meta_ref[g]
        entries = meta[:, :list_len]
        length = meta[:, list_len : list_len + 1]
        full, tail = length // page, length % page
        matches = em_ref[t, pl.ds(g, 1), :]
        for p in range(per_owner):
            same = entries == matches[:, p : p + 1]
            whole = jnp.sum(jnp.where(same & (lane_j < full), 1.0, 0.0), axis=1, keepdims=True)
            part = jnp.sum(jnp.where(same & (lane_j == full), 1.0, 0.0), axis=1, keepdims=True)
            count = whole + jnp.where(lane_t < tail, part, 0.0)
            start = pl.multiple_of((t * per_owner + p) * page, page)
            mask_ref[pl.ds(pl.multiple_of(g * rows, 8), rows), pl.ds(start, page)] = jnp.where(
                count > 0.0, jnp.log2(jnp.maximum(count, 1.0)), DEAD
            )
        return carry

    lax.fori_loop(0, groups * owners, build, 0)
    st_ref[...] = jnp.zeros(st_ref.shape, jnp.float32)

    g_block = max(1, min(groups, 256 // rows))
    row_block = g_block * rows
    blocks = groups // g_block
    owner_chunk = max(1, min(owners, 2048 // (per_owner * page)))
    chunk = owner_chunk * per_owner * page
    lane_s = lax.broadcasted_iota(jnp.int32, (row_block, st_ref.shape[2]), 1)

    for k in range(kv_heads):
        kv_cols = slice(k * HEAD_SIZE, (k + 1) * HEAD_SIZE)

        def one(step, carry):
            block, head = step // per_kv, k * per_kv + step % per_kv
            g0 = block * g_block
            head_cols = pl.ds(pl.multiple_of(head * HEAD_SIZE, HEAD_SIZE), HEAD_SIZE)
            q = q_ref[pl.ds(g0, g_block), :, head_cols].reshape(row_block, HEAD_SIZE)
            top = None
            for c in range(owners // owner_chunk):
                own = slice(c * owner_chunk, (c + 1) * owner_chunk)
                keys = pages_ref[own, :, 0, :, kv_cols].reshape(chunk, HEAD_SIZE)
                values = pages_ref[own, :, 1, :, kv_cols].reshape(chunk, HEAD_SIZE)
                s = lax.dot_general(
                    q, keys, (((1,), (1,)), ((), ())), preferred_element_type=jnp.float32
                )
                s = s * SCALE + mask_ref[
                    pl.ds(pl.multiple_of(block * row_block, 8), row_block),
                    c * chunk : (c + 1) * chunk,
                ]
                here = jnp.max(s, axis=1, keepdims=True)
                new_top = here if top is None else jnp.maximum(top, here)
                e = jnp.exp2(s - new_top)
                total = jnp.sum(e, axis=1, keepdims=True)
                mixed = jnp.dot(
                    e.astype(jnp.bfloat16), values, preferred_element_type=jnp.float32
                )
                if top is None:
                    denom, acc = total, mixed
                else:
                    fade = jnp.exp2(top - new_top)
                    denom, acc = denom * fade + total, acc * fade + mixed
                top = new_top
            o_ref[pl.ds(g0, g_block), :, head_cols] = acc.astype(jnp.bfloat16).reshape(
                g_block, rows, HEAD_SIZE
            )
            old = st_ref[pl.ds(g0, g_block)].reshape(row_block, st_ref.shape[2])
            new = jnp.where(lane_s == head, top, jnp.where(lane_s == head + heads, denom, old))
            st_ref[pl.ds(g0, g_block)] = new.reshape(g_block, rows, st_ref.shape[2])
            return carry

        lax.fori_loop(0, per_kv * blocks, one, 0)


def return_kernel(o_ref, st_ref, o_all, st_all, sems_a, sems_b, sems_c, sems_d, own_sems):
    meet(("grp",))
    copies = spread("grp", lambda g: o_ref.at[g], lambda g: o_all.at[g], sems_a, sems_b, own_sems.at[0])
    copies += spread("grp", lambda g: st_ref.at[g], lambda g: st_all.at[g], sems_c, sems_d, own_sems.at[1])
    for copy in copies:
        copy.wait()


def merge(q_ref, new_ref, o_all, st_all, mix_ref):
    groups, rows, cols = o_all.shape
    heads = cols // HEAD_SIZE
    per_kv = heads // (new_ref.shape[2] // HEAD_SIZE)
    for h in range(heads):
        k = h // per_kv
        head_cols = slice(h * HEAD_SIZE, (h + 1) * HEAD_SIZE)
        kv_cols = slice(k * HEAD_SIZE, (k + 1) * HEAD_SIZE)
        new_key = new_ref[0, :, kv_cols].astype(jnp.float32)
        new_value = new_ref[1, :, kv_cols].astype(jnp.float32)
        own = jnp.sum(q_ref[:, head_cols].astype(jnp.float32) * new_key, axis=1, keepdims=True) * SCALE
        tops = [st_all[g, :, h : h + 1] for g in range(groups)]
        top = functools.reduce(jnp.maximum, tops, own)
        own = jnp.exp2(own - top)
        denom, acc = own, own * new_value
        for g in range(groups):
            fade = jnp.exp2(tops[g] - top)
            denom = denom + fade * st_all[g, :, heads + h : heads + h + 1]
            acc = acc + fade * o_all[g, :, head_cols].astype(jnp.float32)
        mix_ref[:, head_cols] = (acc / denom).astype(jnp.bfloat16)


def project_kernel(q_ref, new_ref, o_all, st_all, w_ref, out_ref, mix_ref):
    @pl.when(pl.program_id(0) == 0)
    def _():
        merge(q_ref, new_ref, o_all, st_all, mix_ref)

    out_ref[0] = jnp.dot(
        mix_ref[...], w_ref[...], preferred_element_type=jnp.float32
    ).astype(jnp.bfloat16)


def sum_kernel(part_ref, out_ref, parts, sems_a, sems_b, own_sem):
    meet(("tp",))
    copies = spread("tp", lambda t: part_ref.at[t], lambda t: parts.at[t], sems_a, sems_b, own_sem)
    for copy in copies:
        copy.wait()
    total = parts[0].astype(jnp.float32)
    for t in range(1, parts.shape[0]):
        total = total + parts[t].astype(jnp.float32)
    out_ref[...] = total.astype(jnp.bfloat16)


def per_device(
    queries, newest_key_value, kv_pages, fetch_slots, block_table, prefix_len, out_weight
):
    T = lax.axis_size("tp")
    G = lax.axis_size("grp")
    tp_rank = lax.axis_index("tp")
    owner = lax.axis_index("grp") * T + tp_rank
    rows, cols = queries.shape
    heads = cols // HEAD_SIZE
    kv_dev = max(1, heads // GROUP_WIDTH)
    width = kv_dev * HEAD_SIZE
    pages_dev, _, page, _ = kv_pages.shape
    list_len = block_table.shape[1]
    limit = fetch_slots.shape[2]
    model = out_weight.shape[1]
    dma = pltpu.SemaphoreType.DMA

    meta = jnp.concatenate([block_table, prefix_len[:, None]], axis=1)
    meta = jnp.pad(meta, ((0, 0), (0, 128 - list_len - 1)))
    slots = fetch_slots.reshape(G, limit)
    hit = slots[:, None, :] == jnp.arange(pages_dev)[None, :, None]
    entry = owner * limit + jnp.arange(limit, dtype=jnp.int32)
    em = jnp.max(jnp.where(hit, entry[None, None, :], -1), axis=2).astype(jnp.int32)
    g_pad = -(-G // 8) * 8
    em = jnp.pad(em, ((0, g_pad - G), (0, 128 - pages_dev)), constant_values=-1)

    q_all, pages_all, meta_all, em_all = pl.pallas_call(
        functools.partial(fetch_kernel, heads, width),
        out_shape=(
            jax.ShapeDtypeStruct((G, rows, cols), jnp.bfloat16),
            jax.ShapeDtypeStruct((T, pages_dev, 2, page, width), jnp.bfloat16),
            jax.ShapeDtypeStruct((G, rows, 128), jnp.int32),
            jax.ShapeDtypeStruct((T, g_pad, 128), jnp.int32),
        ),
        in_specs=[ANY_SPEC] * 4,
        out_specs=(VMEM_SPEC,) * 4,
        scratch_shapes=[dma((T,)), dma((T,)), dma((G,)), dma((G,)), dma((G,)), dma((G,)), dma((T,)), dma((T,)), dma((4,))],
        compiler_params=pltpu.CompilerParams(
            collective_id=0, has_side_effects=True, vmem_limit_bytes=VMEM_LIMIT
        ),
        name="fetch",
    )(queries, kv_pages, meta, em)

    o_part, st_part = pl.pallas_call(
        functools.partial(attend_kernel, list_len),
        out_shape=(
            jax.ShapeDtypeStruct((G, rows, cols), jnp.bfloat16),
            jax.ShapeDtypeStruct((G, rows, 128), jnp.float32),
        ),
        in_specs=[VMEM_SPEC] * 4,
        out_specs=(VMEM_SPEC,) * 2,
        scratch_shapes=[pltpu.VMEM((G * rows, T * pages_dev * page), jnp.float32)],
        compiler_params=pltpu.CompilerParams(vmem_limit_bytes=VMEM_LIMIT),
        name="attend",
    )(q_all, pages_all, meta_all, em_all)

    o_all, st_all = pl.pallas_call(
        return_kernel,
        out_shape=(
            jax.ShapeDtypeStruct((G, rows, cols), jnp.bfloat16),
            jax.ShapeDtypeStruct((G, rows, 128), jnp.float32),
        ),
        in_specs=[ANY_SPEC] * 2,
        out_specs=(VMEM_SPEC,) * 2,
        scratch_shapes=[dma((G,)), dma((G,)), dma((G,)), dma((G,)), dma((2,))],
        compiler_params=pltpu.CompilerParams(
            collective_id=1, has_side_effects=True, vmem_limit_bytes=VMEM_LIMIT
        ),
        name="give_back",
    )(o_part, st_part)

    kv_first = (tp_rank * heads // GROUP_WIDTH) * HEAD_SIZE
    newest = lax.dynamic_slice_in_dim(newest_key_value, kv_first, width, 2).transpose(1, 0, 2)
    share = model // T
    block = min(1024, share)
    per_share = share // block
    depth = out_weight.shape[0]
    parts = pl.pallas_call(
        project_kernel,
        out_shape=jax.ShapeDtypeStruct((T, rows, share), jnp.bfloat16),
        grid=(model // block,),
        in_specs=[
            pl.BlockSpec((rows, cols), lambda j: (0, 0)),
            pl.BlockSpec((2, rows, width), lambda j: (0, 0, 0)),
            pl.BlockSpec((G, rows, cols), lambda j: (0, 0, 0)),
            pl.BlockSpec((G, rows, 128), lambda j: (0, 0, 0)),
            pl.BlockSpec((depth, block), lambda j: (0, j)),
        ],
        out_specs=pl.BlockSpec((1, rows, block), lambda j: (j // per_share, 0, j % per_share)),
        scratch_shapes=[pltpu.VMEM((rows, cols), jnp.bfloat16)],
        compiler_params=pltpu.CompilerParams(vmem_limit_bytes=VMEM_LIMIT),
        name="project",
    )(queries, newest, o_all, st_all, out_weight)

    return pl.pallas_call(
        sum_kernel,
        out_shape=jax.ShapeDtypeStruct((rows, share), jnp.bfloat16),
        in_specs=[ANY_SPEC],
        out_specs=VMEM_SPEC,
        scratch_shapes=[pltpu.VMEM((T, rows, share), jnp.bfloat16), dma((T,)), dma((T,)), dma],
        compiler_params=pltpu.CompilerParams(
            collective_id=2, has_side_effects=True, vmem_limit_bytes=VMEM_LIMIT
        ),
        name="sum_up",
    )(parts)


def solution(mesh):
    in_specs = (
        P(("rep", "grp"), "tp"),
        P(("rep", "grp"), None, None),
        P(("rep", "grp", "tp"), None, None, None),
        P("rep", ("grp", "tp"), None),
        P(("rep", "grp"), None),
        P(("rep", "grp")),
        P("tp", None),
    )
    out_specs = P(("rep", "grp"), "tp")
    return jax.shard_map(
        per_device, mesh=mesh, in_specs=in_specs, out_specs=out_specs, check_vma=False
    )
```

time: 488 us -> 127 us (0.26)
  local copies, waits for them, and re-layouts: 256 us -> 3.66 us
  Pallas kernels: 0 us -> 122 us
  waiting for transfers between devices: 122 us -> 0 us
  matrix products: 67.7 us -> 0 us
  other arithmetic: 15.8 us -> 1.52 us
  between operations: 13.5 us -> 0.04 us
  starting transfers between devices: 7.51 us -> 0 us
    pallas_call x0 -> x5, Pallas kernels: none -> 122 us  [the longest x1 32.2 us: per_device(): pl.pallas_call(functools.partial(fetch_kernel, heads, width), out_shape=(...]
    squeeze x24 -> x0, local copies, waits for them, and re-layouts: 110 us -> none  [the longest x8 55.2 us: attend(): gathered[:, :, 1]]
    gather x13 -> x0, local copies, waits for them, and re-layouts: 88 us -> none  [the longest x8 61 us: attend(): gathered = fetched[table_block]]
    all_to_all x1 -> x0, waiting for transfers between devices: 76.9 us -> none  [per_device(): lax.all_to_all(outgoing, ('grp', 'tp'), split_axis=0, concat_axis=0, tile...]
    dot_general x25 -> x0, matrix products: 67.7 us -> none  [the longest x8 27.8 us: attend(): jnp.einsum('bkqd,bpkd->bkqp', query_tile, key_matrix, preferred_element_t...]
    slice x8 -> x0, local copies, waits for them, and re-layouts: 47.7 us -> none  [attend(): gathered[:, :, 0]]
    reduce_scatter x1 -> x0, waiting for transfers between devices: 44.9 us -> none  [per_device(): lax.psum_scatter(partial_out, 'tp', scatter_dimension=1, tiled=True)]
    all_to_all x1 -> x0, starting transfers between devices: 7.48 us -> none  [per_device(): lax.all_to_all(outgoing, ('grp', 'tp'), split_axis=0, concat_axis=0, tile...]
  transfers between devices with their start and end apart: 2 -> 0, of which waited for: 2 -> 0; matrix products, arithmetic and copies ran while one was open for 0% -> 0% of each run, Pallas kernels for 0% -> 0%
where the time goes in v1:
time: 127 us
  Pallas kernels  122 us (96%)
  local copies, waits for them, and re-layouts  3.66 us (3%)
  other arithmetic  1.52 us (1%)
    pallas_call x1, Pallas kernels, per_device(): pl.pallas_call(functools.partial(fetch_kernel, heads, width), out_shape=(...  32.2 us
    pallas_call x1, Pallas kernels, per_device(): pl.pallas_call(return_kernel, out_shape=(jax.ShapeDtypeStruct((G, rows, c...  28.4 us
    pallas_call x1, Pallas kernels, per_device(): pl.pallas_call(functools.partial(attend_kernel, list_len), out_shape=(jax...  24.8 us
    pallas_call x1, Pallas kernels, per_device(): pl.pallas_call(project_kernel, out_shape=jax.ShapeDtypeStruct((T, rows, s...  19.6 us
    pallas_call x1, Pallas kernels, per_device(): pl.pallas_call(sum_kernel, out_shape=jax.ShapeDtypeStruct((rows, share),...  16.7 us

profile of v1, /device:TPU:1, one launch (start us, length us, event | category | flops | bytes accessed | tf_op | source)
XLA Modules:
  0.0 126.9 jit_solution(2853732759045589640)
XLA Ops:
  0.0 0.0 copy-start
  0.0 0.8 select_reduce_fusion
  0.8 0.6 pad.9.em_ref
  1.4 0.7 pad_add_fusion
  2.1 0.1 copy.16
  2.2 0.6 pad.8.meta_ref
  2.8 0.0 copy-done
  2.9 0.6 copy.19
  3.5 32.2 %fetch.1 = (bf16[4,64,2048]{2,1,0:T(8,128)(2,1)}, bf16[4,4,2,128,256]{4,3,2,1,0:T(8,128)(2,1)}, s32[4,64,128]{2,1,0:T(8,128)}, s32[4,8,128]{2,1,0:T(8,128)}) custom-call(bf16[64,2048]{1,0:T(8,128)(2,1)} %q_ref.3, bf16[4,2,128,1024]{3,2,1,0:T(8,128)(2,1)} %kv_ref.1, s32[64,128]{1,0:T(8,128)} %pad.8.meta_ref, s32[8,128]{1,0:T(8,128)} %pad.9.em_ref), custom_call_target="tpu_custom_call" | custom-call | tf_op jit(solution)/shard_map/fetch/pallas_call | solution.py:238
  35.7 24.8 %attend.1 = (bf16[4,64,2048]{2,1,0:T(8,128)(2,1)}, f32[4,64,128]{2,1,0:T(8,128)}) custom-call(bf16[4,64,2048]{2,1,0:T(8,128)(2,1)} %get-tuple-element.13.q_ref, bf16[4,4,2,128,256]{4,3,2,1,0:T(8,128)(2,1)} %get-tuple-element.14.pages_ref, s32[4,64,128]{2,1,0:T(8,128)} %get-tuple-element.15.meta_ref, s32[4,8,128]{2,1,0:T(8,128)} %get-tuple-element.16.em_ref), custom_call_target="tpu_custom_call" | custom-call | tf_op jit(solution)/shard_map/attend/pallas_call | solution.py:255
  60.5 28.4 %give_back.1 = (bf16[4,64,2048]{2,1,0:T(8,128)(2,1)}, f32[4,64,128]{2,1,0:T(8,128)}) custom-call(bf16[4,64,2048]{2,1,0:T(8,128)(2,1)} %get-tuple-element.17.o_ref, f32[4,64,128]{2,1,0:T(8,128)} %get-tuple-element.18.st_ref), custom_call_target="tpu_custom_call" | custom-call | tf_op jit(solution)/shard_map/give_back/pallas_call | solution.py:268
  88.9 19.6 %project.1.part_ref = bf16[4,64,2048]{2,1,0:T(8,128)(2,1)} custom-call(bf16[64,2048]{1,0:T(8,128)(2,1)} %q_ref.3, bf16[2,64,256]{2,1,0:T(8,128)(2,1)} %bitcast.5, bf16[4,64,2048]{2,1,0:T(8,128)(2,1)} %get-tuple-element.19.o_all, f32[4,64,128]{2,1,0:T(8,128)} %get-tuple-element.20.st_all, bf16[2048,8192]{1,0:T(8,128)(2,1)} %w_ref.1), custom_call_target="tpu_custom_call" | custom-call | tf_op jit(solution)/shard_map/project/pallas_call | solution.py:289
  108.5 16.7 %sum_up.1 = bf16[64,2048]{1,0:T(8,128)(2,1)} custom-call(bf16[4,64,2048]{2,1,0:T(8,128)(2,1)} %project.1.part_ref), custom_call_target="tpu_custom_call" | custom-call | tf_op jit(solution)/shard_map/sum_up/pallas_call | solution.py:306
  125.2 1.7 %copy.21 = bf16[64,2048]{1,0:T(8,128)(2,1)} copy(bf16[64,2048]{1,0:T(8,128)(2,1)} %sum_up.1) | data formatting | bytes 524288
  (2 shorter events, 0.1 us)
Async XLA Ops:
  0.0 2.8 %copy-start = (bf16[64,2,1024]{2,1,0:T(2,128)(2,1)S(1)}, bf16[64,2,1024]{2,1,0:T(2,128)(2,1)}, u32[]{:S(2)}) copy-start(bf16[64,2,1024]{2,1,0:T(2,128)(2,1)} %param.8) | copy-start | bytes 786436

commit v2 on v0

v2 whole, which is shorter than its diff:
```python
import functools
import math

import jax
import jax.numpy as jnp
from jax import lax
from jax.experimental import pallas as pl
from jax.experimental.pallas import tpu as pltpu
from jax.sharding import PartitionSpec as P

QUERY_HEADS = 64
KEY_VALUE_HEADS = 8
HEAD_SIZE = 128
GROUP_WIDTH = QUERY_HEADS // KEY_VALUE_HEADS
DEAD = -1e30
SCALE = math.log2(math.e) / math.sqrt(HEAD_SIZE)
MESH = pl.DeviceIdType.MESH
VMEM_LIMIT = 60 * 1024 * 1024

VMEM_SPEC = pl.BlockSpec(memory_space=pltpu.VMEM)
ANY_SPEC = pl.BlockSpec(memory_space=pl.ANY)


def routes(axis):
    count = lax.axis_size(axis)
    me = lax.axis_index(axis)
    if axis == "tp" and count % 2 == 0:
        pair, core = me // 2, me % 2
        pairs = count // 2
        steps = [(i, b) for i in range(1, pairs) for b in range(2)] + [(0, 1)]
        return [lax.rem(pair + i, pairs) * 2 + lax.rem(core + b, 2) for i, b in steps]
    return [lax.rem(me + d, count) for d in range(1, count)]


def meet(axes):
    barrier = pltpu.get_barrier_semaphore()
    total = 0
    for axis in axes:
        for target in routes(axis):
            pl.semaphore_signal(barrier, inc=1, device_id={axis: target}, device_id_type=MESH)
            total += 1
    pl.semaphore_wait(barrier, total)


def remote(source, dest, send_sem, recv_sem, axis, target):
    return pltpu.make_async_remote_copy(
        src_ref=source,
        dst_ref=dest,
        send_sem=send_sem,
        recv_sem=recv_sem,
        device_id={axis: target},
        device_id_type=MESH,
    )


def spread(axis, source_of, dest, send_sem, recv_sem, own_sem):
    me = lax.axis_index(axis)
    copies = []
    for i, target in enumerate(routes(axis)):
        copies.append(
            remote(source_of(target), dest, send_sem.at[i], recv_sem.at[i], axis, target)
        )
    copies.append(pltpu.make_async_copy(source_of(me), dest, own_sem))
    for copy in copies:
        copy.start()
    return copies


def wait_all(copies):
    for copy in copies:
        copy.wait()


def build_mask(list_len, groups, rows, owners, per_owner, page, meta_ref, em_ref, mask_ref):
    lane_j = lax.broadcasted_iota(jnp.int32, (rows, list_len), 1)
    lane_t = lax.broadcasted_iota(jnp.int32, (rows, page), 1)

    def build(step, carry):
        g, t = step // owners, step % owners
        meta = meta_ref[g]
        entries = meta[:, :list_len]
        length = meta[:, list_len : list_len + 1]
        full, tail = length // page, length % page
        matches = em_ref[t, pl.ds(g, 1), :]
        for p in range(per_owner):
            same = entries == matches[:, p : p + 1]
            whole = jnp.sum(jnp.where(same & (lane_j < full), 1.0, 0.0), axis=1, keepdims=True)
            part = jnp.sum(jnp.where(same & (lane_j == full), 1.0, 0.0), axis=1, keepdims=True)
            count = whole + jnp.where(lane_t < tail, part, 0.0)
            start = pl.multiple_of((t * per_owner + p) * page, page)
            mask_ref[pl.ds(pl.multiple_of(g * rows, 8), rows), pl.ds(start, page)] = jnp.where(
                count > 0.0, jnp.log2(jnp.maximum(count, 1.0)), DEAD
            )
        return carry

    lax.fori_loop(0, groups * owners, build, 0)


def merge(q_ref, new_ref, o_parts, st_parts, mix_ref):
    rows, cols = mix_ref.shape
    heads = cols // HEAD_SIZE
    per_kv = heads // (new_ref.shape[2] // HEAD_SIZE)
    for h in range(heads):
        k = h // per_kv
        head_cols = slice(h * HEAD_SIZE, (h + 1) * HEAD_SIZE)
        kv_cols = slice(k * HEAD_SIZE, (k + 1) * HEAD_SIZE)
        new_key = new_ref[0, :, kv_cols].astype(jnp.float32)
        new_value = new_ref[1, :, kv_cols].astype(jnp.float32)
        own = jnp.sum(q_ref[:, head_cols].astype(jnp.float32) * new_key, axis=1, keepdims=True) * SCALE
        tops = [st[:, h : h + 1] for st in st_parts]
        top = functools.reduce(jnp.maximum, tops, own)
        own = jnp.exp2(own - top)
        denom, acc = own, own * new_value
        for part, st, part_top in zip(o_parts, st_parts, tops):
            fade = jnp.exp2(part_top - top)
            denom = denom + fade * st[:, heads + h : heads + h + 1]
            acc = acc + fade * part[:, head_cols].astype(jnp.float32)
        mix_ref[:, head_cols] = (acc / denom).astype(jnp.bfloat16)


def step_kernel(
    list_len, q_in, kv_in, meta_in, em_in, new_ref, w_in, out_ref,
    q_ref, pages_ref, meta_ref, em_ref, mask_ref, o_ref, st_ref, o_got, st_got,
    w_ref, mix_ref, part_ref, part_got, own_part,
    tp_send, tp_recv, grp_send, grp_recv, own_sems, w_sems,
):
    groups, rows, cols = q_ref.shape
    owners, kv_heads, per_owner, _, page, _ = pages_ref.shape
    heads = cols // HEAD_SIZE
    per_kv = heads // kv_heads
    my_group, my_tp = lax.axis_index("grp"), lax.axis_index("tp")
    model = w_in.shape[1]
    share = model // owners

    meet(("tp", "grp"))

    small = spread("tp", lambda t: em_in, em_ref.at[my_tp], tp_send.at[0], tp_recv.at[0], own_sems.at[0])
    small += spread("grp", lambda g: meta_in, meta_ref.at[my_group], grp_send.at[0], grp_recv.at[0], own_sems.at[1])
    arrivals = []
    for k in range(kv_heads):

        def columns(t):
            first = (t * heads // GROUP_WIDTH + k) * HEAD_SIZE
            return kv_in.at[:, :, :, pl.ds(pl.multiple_of(first, HEAD_SIZE), HEAD_SIZE)]

        span = slice(k * per_kv * HEAD_SIZE, (k + 1) * per_kv * HEAD_SIZE)
        n = 1 + k
        copies = spread("tp", columns, pages_ref.at[my_tp, k], tp_send.at[n], tp_recv.at[n], own_sems.at[2 * n])
        copies += spread(
            "grp", lambda g: q_in.at[:, span], q_ref.at[my_group, :, span],
            grp_send.at[n], grp_recv.at[n], own_sems.at[2 * n + 1],
        )
        arrivals.append(copies)

    targets = routes("tp") + [my_tp]
    w_copies = []
    for i, t in enumerate(targets):
        span = pl.ds(pl.multiple_of(t * share, 128), share)
        w_copies.append(pltpu.make_async_copy(w_in.at[:, span], w_ref.at[i], w_sems.at[i]))
        w_copies[-1].start()

    wait_all(small)
    build_mask(list_len, groups, rows, owners, per_owner, page, meta_ref, em_ref, mask_ref)
    st_ref[...] = jnp.zeros(st_ref.shape, jnp.float32)

    g_block = max(1, min(groups, 256 // rows))
    row_block = g_block * rows
    blocks = groups // g_block
    owner_chunk = max(1, min(owners, 2048 // (per_owner * page)))
    chunk = owner_chunk * per_owner * page
    lane_s = lax.broadcasted_iota(jnp.int32, (row_block, st_ref.shape[2]), 1)
    unroll = 2 if per_kv % 2 == 0 else 1
    piece = unroll * HEAD_SIZE
    group_targets = routes("grp")
    o_slot, st_slot = 1 + kv_heads, 2 + kv_heads

    def one(k, block, head):
        g0 = block * g_block
        head_cols = pl.ds(pl.multiple_of(head * HEAD_SIZE, HEAD_SIZE), HEAD_SIZE)
        q = q_ref[pl.ds(g0, g_block), :, head_cols].reshape(row_block, HEAD_SIZE)
        top = None
        for c in range(owners // owner_chunk):
            own = slice(c * owner_chunk, (c + 1) * owner_chunk)
            keys = pages_ref[own, k, :, 0].reshape(chunk, HEAD_SIZE)
            values = pages_ref[own, k, :, 1].reshape(chunk, HEAD_SIZE)
            s = lax.dot_general(
                q, keys, (((1,), (1,)), ((), ())), preferred_element_type=jnp.float32
            )
            s = s * SCALE + mask_ref[
                pl.ds(pl.multiple_of(block * row_block, 8), row_block),
                c * chunk : (c + 1) * chunk,
            ]
            here = jnp.max(s, axis=1, keepdims=True)
            new_top = here if top is None else jnp.maximum(top, here)
            e = jnp.exp2(s - new_top)
            total = jnp.sum(e, axis=1, keepdims=True)
            mixed = jnp.dot(e.astype(jnp.bfloat16), values, preferred_element_type=jnp.float32)
            if top is None:
                denom, acc = total, mixed
            else:
                fade = jnp.exp2(top - new_top)
                denom, acc = denom * fade + total, acc * fade + mixed
            top = new_top
        o_ref[pl.ds(g0, g_block), :, head_cols] = acc.astype(jnp.bfloat16).reshape(
            g_block, rows, HEAD_SIZE
        )
        old = st_ref[pl.ds(g0, g_block)].reshape(row_block, st_ref.shape[2])
        new = jnp.where(lane_s == head, top, jnp.where(lane_s == head + heads, denom, old))
        st_ref[pl.ds(g0, g_block)] = new.reshape(g_block, rows, st_ref.shape[2])

    for k in range(kv_heads):
        wait_all(arrivals[k])

        def some(step, carry):
            head0 = k * per_kv + step * unroll

            def rows_of(block, inner):
                for u in range(unroll):
                    one(k, block, head0 + u)
                return inner

            if blocks == 1:
                rows_of(0, 0)
            else:
                lax.fori_loop(0, blocks, rows_of, 0)
            span = pl.ds(pl.multiple_of(head0 * HEAD_SIZE, HEAD_SIZE), piece)
            for i, g in enumerate(group_targets):
                remote(
                    o_ref.at[g, :, span], o_got.at[i, :, span],
                    grp_send.at[o_slot, i], grp_recv.at[o_slot, i], "grp", g,
                ).start()
            return carry

        lax.fori_loop(0, per_kv // unroll, some, 0)

    stats = []
    for i, g in enumerate(group_targets):
        stats.append(
            remote(
                st_ref.at[g], st_got.at[i],
                grp_send.at[st_slot, i], grp_recv.at[st_slot, i], "grp", g,
            )
        )
        stats[-1].start()
    for i, g in enumerate(group_targets):
        remote(
            o_ref.at[g], o_got.at[i],
            grp_send.at[o_slot, i], grp_recv.at[o_slot, i], "grp", g,
        ).wait()
    wait_all(stats)

    parts = [o_got.at[i] for i in range(groups - 1)] + [o_ref.at[my_group]]
    st_parts = [st_got.at[i] for i in range(groups - 1)] + [st_ref.at[my_group]]
    merge(q_ref.at[my_group], new_ref, parts, st_parts, mix_ref)

    block = min(512, share)
    sent = []
    slot = 1 + kv_heads
    for i, t in enumerate(targets):
        w_copies[i].wait()

        def project(s, carry):
            span = pl.ds(pl.multiple_of(s * block, 128), block)
            made = jnp.dot(mix_ref[...], w_ref[i, :, span], preferred_element_type=jnp.float32)
            if i < owners - 1:
                part_ref[i, :, span] = made.astype(jnp.bfloat16)
            else:
                own_part[:, span] = made
            return carry

        lax.fori_loop(0, share // block, project, 0)
        if i < owners - 1:
            sent.append(
                remote(
                    part_ref.at[i], part_got.at[i],
                    tp_send.at[slot, i], tp_recv.at[slot, i], "tp", t,
                )
            )
            sent[-1].start()
    total = own_part[...]
    for i in reversed(range(owners - 1)):
        sent[i].wait()
        total = total + part_got[i].astype(jnp.float32)
    out_ref[...] = total.astype(jnp.bfloat16)


def per_device(
    queries, newest_key_value, kv_pages, fetch_slots, block_table, prefix_len, out_weight
):
    T = lax.axis_size("tp")
    G = lax.axis_size("grp")
    tp_rank = lax.axis_index("tp")
    owner = lax.axis_index("grp") * T + tp_rank
    rows, cols = queries.shape
    heads = cols // HEAD_SIZE
    kv_dev = max(1, heads // GROUP_WIDTH)
    width = kv_dev * HEAD_SIZE
    pages_dev, _, page, _ = kv_pages.shape
    list_len = block_table.shape[1]
    limit = fetch_slots.shape[2]
    model = out_weight.shape[1]
    dma = pltpu.SemaphoreType.DMA

    meta = jnp.concatenate([block_table, prefix_len[:, None]], axis=1)
    meta = jnp.pad(meta, ((0, 0), (0, 128 - list_len - 1)))
    slots = fetch_slots.reshape(G, limit)
    hit = slots[:, None, :] == jnp.arange(pages_dev)[None, :, None]
    entry = owner * limit + jnp.arange(limit, dtype=jnp.int32)
    em = jnp.max(jnp.where(hit, entry[None, None, :], -1), axis=2).astype(jnp.int32)
    g_pad = -(-G // 8) * 8
    em = jnp.pad(em, ((0, g_pad - G), (0, 128 - pages_dev)), constant_values=-1)

    kv_first = (tp_rank * heads // GROUP_WIDTH) * HEAD_SIZE
    newest = lax.dynamic_slice_in_dim(newest_key_value, kv_first, width, 2).transpose(1, 0, 2)
    share = model // T
    bf16, f32, i32 = jnp.bfloat16, jnp.float32, jnp.int32
    vmem = pltpu.VMEM
    return pl.pallas_call(
        functools.partial(step_kernel, list_len),
        out_shape=jax.ShapeDtypeStruct((rows, share), bf16),
        in_specs=[ANY_SPEC] * 4 + [VMEM_SPEC, ANY_SPEC],
        out_specs=VMEM_SPEC,
        scratch_shapes=[
            vmem((G, rows, cols), bf16),
            vmem((T, kv_dev, pages_dev, 2, page, HEAD_SIZE), bf16),
            vmem((G, rows, 128), i32),
            vmem((T, g_pad, 128), i32),
            vmem((G * rows, T * pages_dev * page), f32),
            vmem((G, rows, cols), bf16),
            vmem((G, rows, 128), f32),
            vmem((G - 1, rows, cols), bf16),
            vmem((G - 1, rows, 128), f32),
            vmem((T, out_weight.shape[0], share), bf16),
            vmem((rows, cols), bf16),
            vmem((T - 1, rows, share), bf16),
            vmem((T - 1, rows, share), bf16),
            vmem((rows, share), f32),
            dma((2 + kv_dev, T - 1)),
            dma((2 + kv_dev, T - 1)),
            dma((3 + kv_dev, G - 1)),
            dma((3 + kv_dev, G - 1)),
            dma((2 + 2 * kv_dev,)),
            dma((T,)),
        ],
        compiler_params=pltpu.CompilerParams(
            collective_id=0, has_side_effects=True, vmem_limit_bytes=VMEM_LIMIT
        ),
        name="decode_step",
    )(queries, kv_pages, meta, em, newest, out_weight)


def solution(mesh):
    in_specs = (
        P(("rep", "grp"), "tp"),
        P(("rep", "grp"), None, None),
        P(("rep", "grp", "tp"), None, None, None),
        P("rep", ("grp", "tp"), None),
        P(("rep", "grp"), None),
        P(("rep", "grp")),
        P("tp", None),
    )
    out_specs = P(("rep", "grp"), "tp")
    return jax.shard_map(
        per_device, mesh=mesh, in_specs=in_specs, out_specs=out_specs, check_vma=False
    )
```

time: 488 us -> 81.5 us (0.17)
  local copies, waits for them, and re-layouts: 256 us -> 3.66 us
  waiting for transfers between devices: 122 us -> 0 us
  Pallas kernels: 0 us -> 75.3 us
  matrix products: 67.7 us -> 0 us
  other arithmetic: 15.8 us -> 1.52 us
  between operations: 13.5 us -> 0.02 us
  starting transfers between devices: 7.51 us -> 0 us
    squeeze x24 -> x0, local copies, waits for them, and re-layouts: 110 us -> none  [the longest x8 55.2 us: attend(): gathered[:, :, 1]]
    gather x13 -> x0, local copies, waits for them, and re-layouts: 88 us -> none  [the longest x8 61 us: attend(): gathered = fetched[table_block]]
    all_to_all x1 -> x0, waiting for transfers between devices: 76.9 us -> none  [per_device(): lax.all_to_all(outgoing, ('grp', 'tp'), split_axis=0, concat_axis=0, tile...]
    pallas_call x0 -> x1, Pallas kernels: none -> 75.3 us  [per_device(): pl.pallas_call(functools.partial(step_kernel, list_len), out_shape=jax.Sh...]
    dot_general x25 -> x0, matrix products: 67.7 us -> none  [the longest x8 27.8 us: attend(): jnp.einsum('bkqd,bpkd->bkqp', query_tile, key_matrix, preferred_element_t...]
    slice x8 -> x0, local copies, waits for them, and re-layouts: 47.7 us -> none  [attend(): gathered[:, :, 0]]
    reduce_scatter x1 -> x0, waiting for transfers between devices: 44.9 us -> none  [per_device(): lax.psum_scatter(partial_out, 'tp', scatter_dimension=1, tiled=True)]
    all_to_all x1 -> x0, starting transfers between devices: 7.48 us -> none  [per_device(): lax.all_to_all(outgoing, ('grp', 'tp'), split_axis=0, concat_axis=0, tile...]
  transfers between devices with their start and end apart: 2 -> 0, of which waited for: 2 -> 0; matrix products, arithmetic and copies ran while one was open for 0% -> 0% of each run, Pallas kernels for 0% -> 0%
where the time goes in v2:
time: 81.5 us; the launch traced here: 80.5 us
  Pallas kernels  75.3 us (92%)
  local copies, waits for them, and re-layouts  3.66 us (4%)
  other arithmetic  1.52 us (2%)
    pallas_call x1, Pallas kernels, per_device(): pl.pallas_call(functools.partial(step_kernel, list_len), out_shape=jax.Sh...  75.3 us
    unnamed x4, local copies, waits for them, and re-layouts  2.31 us

profile of v2, /device:TPU:1, one launch (start us, length us, event | category | flops | bytes accessed | tf_op | source)
XLA Modules:
  0.0 80.5 jit_solution(12936059936832069991)
XLA Ops:
  0.0 0.0 copy-start
  0.0 0.8 select_reduce_fusion
  0.8 0.6 pad.9.em_in
  1.4 0.7 pad_add_fusion
  2.1 0.1 copy.15
  2.2 0.6 pad.8.meta_in
  2.8 0.0 copy-done
  2.9 0.6 copy.19
  3.5 75.3 %decode_step.1 = bf16[64,2048]{1,0:T(8,128)(2,1)} custom-call(bf16[64,2048]{1,0:T(8,128)(2,1)} %q_in.1, bf16[4,2,128,1024]{3,2,1,0:T(8,128)(2,1)} %kv_in.1, s32[64,128]{1,0:T(8,128)} %pad.8.meta_in, s32[8,128]{1,0:T(8,128)} %pad.9.em_in, bf16[2,64,256]{2,1,0:T(8,128)(2,1)} %bitcast.5, bf16[2048,8192]{1,0:T(8,128)(2,1)} %w_in.1), custom_call_target="tpu_custom_call" | custom-call | tf_op jit(solution)/shard_map/decode_step/pallas_call | solution.py:318
  78.8 1.7 %copy.21 = bf16[64,2048]{1,0:T(8,128)(2,1)} copy(bf16[64,2048]{1,0:T(8,128)(2,1)} %decode_step.1) | data formatting | bytes 524288
  (2 shorter events, 0.1 us)
Async XLA Ops:
  0.0 2.8 %copy-start = (bf16[64,2,1024]{2,1,0:T(2,128)(2,1)S(1)}, bf16[64,2,1024]{2,1,0:T(2,128)(2,1)}, u32[]{:S(2)}) copy-start(bf16[64,2,1024]{2,1,0:T(2,128)(2,1)} %param.8) | copy-start | bytes 786436

commit v3 on v2

--- a/solution.py
+++ b/solution.py
@@ -96,12 +96,9 @@
     lax.fori_loop(0, groups * owners, build, 0)
 
 
-def merge(q_ref, new_ref, o_parts, st_parts, mix_ref):
-    rows, cols = mix_ref.shape
-    heads = cols // HEAD_SIZE
-    per_kv = heads // (new_ref.shape[2] // HEAD_SIZE)
-    for h in range(heads):
-        k = h // per_kv
+def merge(k, per_kv, q_ref, new_ref, o_parts, st_parts, mix_ref):
+    heads = mix_ref.shape[1] // HEAD_SIZE
+    for h in range(k * per_kv, (k + 1) * per_kv):
         head_cols = slice(h * HEAD_SIZE, (h + 1) * HEAD_SIZE)
         kv_cols = slice(k * HEAD_SIZE, (k + 1) * HEAD_SIZE)
         new_key = new_ref[0, :, kv_cols].astype(jnp.float32)
@@ -121,7 +118,7 @@
 def step_kernel(
     list_len, q_in, kv_in, meta_in, em_in, new_ref, w_in, out_ref,
     q_ref, pages_ref, meta_ref, em_ref, mask_ref, o_ref, st_ref, o_got, st_got,
-    w_ref, mix_ref, part_ref, part_got, own_part,
+    w_ref, mix_ref, part_ref, part_got, acc_ref,
     tp_send, tp_recv, grp_send, grp_recv, own_sems, w_sems,
 ):
     groups, rows, cols = q_ref.shape
@@ -136,23 +133,63 @@
 
     small = spread("tp", lambda t: em_in, em_ref.at[my_tp], tp_send.at[0], tp_recv.at[0], own_sems.at[0])
     small += spread("grp", lambda g: meta_in, meta_ref.at[my_group], grp_send.at[0], grp_recv.at[0], own_sems.at[1])
-    arrivals = []
+    tp_targets, group_targets = routes("tp"), routes("grp")
+
+    def page_columns(t, k, which):
+        first = (t * heads // GROUP_WIDTH + k) * HEAD_SIZE
+        return kv_in.at[which, :, :, pl.ds(pl.multiple_of(first, HEAD_SIZE), HEAD_SIZE)]
+
+    def page_copies(k, which):
+        return [
+            remote(
+                page_columns(t, k, which), pages_ref.at[my_tp, k, which],
+                tp_send.at[1 + k, i], tp_recv.at[1 + k, i], "tp", t,
+            )
+            for i, t in enumerate(tp_targets)
+        ]
+
+    def query_copies(k):
+        span = slice(k * per_kv * HEAD_SIZE, (k + 1) * per_kv * HEAD_SIZE)
+        return [
+            remote(
+                q_in.at[:, span], q_ref.at[my_group, :, span],
+                grp_send.at[1 + k, i], grp_recv.at[1 + k, i], "grp", g,
+            )
+            for i, g in enumerate(group_targets)
+        ]
+
+    def own_copies(k):
+        span = slice(k * per_kv * HEAD_SIZE, (k + 1) * per_kv * HEAD_SIZE)
+        return [
+            pltpu.make_async_copy(
+                page_columns(my_tp, k, slice(None)), pages_ref.at[my_tp, k], own_sems.at[2 + 2 * k]
+            ),
+            pltpu.make_async_copy(
+                q_in.at[:, span], q_ref.at[my_group, :, span], own_sems.at[3 + 2 * k]
+            ),
+        ]
+
+    def start_all(copies):
+        for copy in copies:
+            copy.start()
+
+    @pl.when(my_tp % 2 == 0)
+    def _():
+        start_all(page_copies(0, slice(None)))
+        start_all(query_copies(0))
+
+    @pl.when(my_tp % 2 == 1)
+    def _():
+        start_all(query_copies(0))
+        start_all(page_copies(0, slice(None)))
+
     for k in range(kv_heads):
-
-        def columns(t):
-            first = (t * heads // GROUP_WIDTH + k) * HEAD_SIZE
-            return kv_in.at[:, :, :, pl.ds(pl.multiple_of(first, HEAD_SIZE), HEAD_SIZE)]
-
-        span = slice(k * per_kv * HEAD_SIZE, (k + 1) * per_kv * HEAD_SIZE)
-        n = 1 + k
-        copies = spread("tp", columns, pages_ref.at[my_tp, k], tp_send.at[n], tp_recv.at[n], own_sems.at[2 * n])
-        copies += spread(
-            "grp", lambda g: q_in.at[:, span], q_ref.at[my_group, :, span],
-            grp_send.at[n], grp_recv.at[n], own_sems.at[2 * n + 1],
-        )
-        arrivals.append(copies)
-
-    targets = routes("tp") + [my_tp]
+        start_all(own_copies(k))
+        if k > 0:
+            start_all(page_copies(k, pl.ds(0, 1)))
+            start_all(query_copies(k))
+
+    targets = tp_targets + [my_tp]
     w_copies = []
     for i, t in enumerate(targets):
         span = pl.ds(pl.multiple_of(t * share, 128), share)
@@ -168,11 +205,20 @@
     blocks = groups // g_block
     owner_chunk = max(1, min(owners, 2048 // (per_owner * page)))
     chunk = owner_chunk * per_owner * page
-    lane_s = lax.broadcasted_iota(jnp.int32, (row_block, st_ref.shape[2]), 1)
+    lane_s = lax.broadcasted_iota(jnp.int32, (row_block, st_ref.shape[3]), 1)
     unroll = 2 if per_kv % 2 == 0 else 1
     piece = unroll * HEAD_SIZE
-    group_targets = routes("grp")
-    o_slot, st_slot = 1 + kv_heads, 2 + kv_heads
+    steps = per_kv // unroll
+
+    def stat_copies(k):
+        st_slot = 1 + 2 * kv_heads + k
+        return [
+            remote(
+                st_ref.at[k, g], st_got.at[k, i],
+                grp_send.at[st_slot, i], grp_recv.at[st_slot, i], "grp", g,
+            )
+            for i, g in enumerate(group_targets)
+        ]
 
     def one(k, block, head):
         g0 = block * g_block
@@ -204,15 +250,22 @@
         o_ref[pl.ds(g0, g_block), :, head_cols] = acc.astype(jnp.bfloat16).reshape(
             g_block, rows, HEAD_SIZE
         )
-        old = st_ref[pl.ds(g0, g_block)].reshape(row_block, st_ref.shape[2])
+        old = st_ref[k, pl.ds(g0, g_block)].reshape(row_block, st_ref.shape[3])
         new = jnp.where(lane_s == head, top, jnp.where(lane_s == head + heads, denom, old))
-        st_ref[pl.ds(g0, g_block)] = new.reshape(g_block, rows, st_ref.shape[2])
+        st_ref[k, pl.ds(g0, g_block)] = new.reshape(g_block, rows, st_ref.shape[3])
 
     for k in range(kv_heads):
-        wait_all(arrivals[k])
+        wait_all(page_copies(k, slice(None)) + query_copies(k) + own_copies(k))
+        o_slot = 1 + kv_heads + k
 
         def some(step, carry):
             head0 = k * per_kv + step * unroll
+            if k + 1 < kv_heads:
+
+                @pl.when(step < per_owner - 1)
+                def _():
+                    start_all(page_copies(k + 1, pl.ds(step + 1, 1)))
+
 
             def rows_of(block, inner):
                 for u in range(unroll):
@@ -231,53 +284,55 @@
                 ).start()
             return carry
 
-        lax.fori_loop(0, per_kv // unroll, some, 0)
-
-    stats = []
-    for i, g in enumerate(group_targets):
-        stats.append(
-            remote(
-                st_ref.at[g], st_got.at[i],
-                grp_send.at[st_slot, i], grp_recv.at[st_slot, i], "grp", g,
-            )
-        )
-        stats[-1].start()
-    for i, g in enumerate(group_targets):
-        remote(
-            o_ref.at[g], o_got.at[i],
-            grp_send.at[o_slot, i], grp_recv.at[o_slot, i], "grp", g,
-        ).wait()
-    wait_all(stats)
-
-    parts = [o_got.at[i] for i in range(groups - 1)] + [o_ref.at[my_group]]
-    st_parts = [st_got.at[i] for i in range(groups - 1)] + [st_ref.at[my_group]]
-    merge(q_ref.at[my_group], new_ref, parts, st_parts, mix_ref)
+        lax.fori_loop(0, steps, some, 0)
+        for p in range(steps + 1, per_owner):
+            if k + 1 < kv_heads:
+                start_all(page_copies(k + 1, pl.ds(p, 1)))
+        start_all(stat_copies(k))
 
     block = min(512, share)
     sent = []
     slot = 1 + kv_heads
-    for i, t in enumerate(targets):
-        w_copies[i].wait()
-
-        def project(s, carry):
-            span = pl.ds(pl.multiple_of(s * block, 128), block)
-            made = jnp.dot(mix_ref[...], w_ref[i, :, span], preferred_element_type=jnp.float32)
-            if i < owners - 1:
-                part_ref[i, :, span] = made.astype(jnp.bfloat16)
-            else:
-                own_part[:, span] = made
-            return carry
-
-        lax.fori_loop(0, share // block, project, 0)
-        if i < owners - 1:
-            sent.append(
-                remote(
-                    part_ref.at[i], part_got.at[i],
-                    tp_send.at[slot, i], tp_recv.at[slot, i], "tp", t,
+    for k in range(kv_heads):
+        span = slice(k * per_kv * HEAD_SIZE, (k + 1) * per_kv * HEAD_SIZE)
+        o_slot = 1 + kv_heads + k
+        for i, g in enumerate(group_targets):
+            remote(
+                o_ref.at[g, :, span], o_got.at[i, :, span],
+                grp_send.at[o_slot, i], grp_recv.at[o_slot, i], "grp", g,
+            ).wait()
+        wait_all(stat_copies(k))
+        parts = [o_got.at[i] for i in range(groups - 1)] + [o_ref.at[my_group]]
+        st_parts = [st_got.at[k, i] for i in range(groups - 1)] + [st_ref.at[k, my_group]]
+        merge(k, per_kv, q_ref.at[my_group], new_ref, parts, st_parts, mix_ref)
+        last = k == kv_heads - 1
+        for i, t in enumerate(targets):
+            if k == 0:
+                w_copies[i].wait()
+
+            def project(step, carry):
+                out = pl.ds(pl.multiple_of(step * block, 128), block)
+                made = jnp.dot(
+                    mix_ref[:, span], w_ref[i, span, out], preferred_element_type=jnp.float32
                 )
-            )
-            sent[-1].start()
-    total = own_part[...]
+                if k > 0:
+                    made = made + acc_ref[i, :, out]
+                if last and i < owners - 1:
+                    part_ref[i, :, out] = made.astype(jnp.bfloat16)
+                else:
+                    acc_ref[i, :, out] = made
+                return carry
+
+            lax.fori_loop(0, share // block, project, 0)
+            if last and i < owners - 1:
+                sent.append(
+                    remote(
+                        part_ref.at[i], part_got.at[i],
+                        tp_send.at[slot, i], tp_recv.at[slot, i], "tp", t,
+                    )
+                )
+                sent[-1].start()
+    total = acc_ref[owners - 1]
     for i in reversed(range(owners - 1)):
         sent[i].wait()
         total = total + part_got[i].astype(jnp.float32)
@@ -327,18 +382,18 @@
             vmem((T, g_pad, 128), i32),
             vmem((G * rows, T * pages_dev * page), f32),
             vmem((G, rows, cols), bf16),
-            vmem((G, rows, 128), f32),
+            vmem((kv_dev, G, rows, 128), f32),
             vmem((G - 1, rows, cols), bf16),
-            vmem((G - 1, rows, 128), f32),
+            vmem((kv_dev, G - 1, rows, 128), f32),
             vmem((T, out_weight.shape[0], share), bf16),
             vmem((rows, cols), bf16),
             vmem((T - 1, rows, share), bf16),
             vmem((T - 1, rows, share), bf16),
-            vmem((rows, share), f32),
+            vmem((T, rows, share), f32),
             dma((2 + kv_dev, T - 1)),
             dma((2 + kv_dev, T - 1)),
-            dma((3 + kv_dev, G - 1)),
-            dma((3 + kv_dev, G - 1)),
+            dma((1 + 3 * kv_dev, G - 1)),
+            dma((1 + 3 * kv_dev, G - 1)),
             dma((2 + 2 * kv_dev,)),
             dma((T,)),
         ],

time: 81.5 us -> 82.3 us (level)
  Pallas kernels: 75.3 us -> 76.8 us
    pallas_call x1, Pallas kernels: 75.3 us -> 76.8 us  [per_device(): pl.pallas_call(functools.partial(step_kernel, list_len), out_shape=jax.Sh...]
where the time goes in v3:
time: 82.3 us; the launch traced here: 82 us
  Pallas kernels  76.8 us (93%)
  local copies, waits for them, and re-layouts  3.66 us (4%)
  other arithmetic  1.52 us (2%)
    pallas_call x1, Pallas kernels, per_device(): pl.pallas_call(functools.partial(step_kernel, list_len), out_shape=jax.Sh...  76.8 us
    unnamed x4, local copies, waits for them, and re-layouts  2.31 us

profile of v3, /device:TPU:1, one launch (start us, length us, event | category | flops | bytes accessed | tf_op | source)
XLA Modules:
  0.0 82.0 jit_solution(3820919448186734248)
XLA Ops:
  0.0 0.0 copy-start
  0.0 0.8 select_reduce_fusion
  0.8 0.6 pad.9.em_in
  1.4 0.7 pad_add_fusion
  2.1 0.1 copy.15
  2.2 0.6 pad.8.meta_in
  2.8 0.0 copy-done
  2.9 0.6 copy.19
  3.5 76.8 %decode_step.1 = bf16[64,2048]{1,0:T(8,128)(2,1)} custom-call(bf16[64,2048]{1,0:T(8,128)(2,1)} %q_in.1, bf16[4,2,128,1024]{3,2,1,0:T(8,128)(2,1)} %kv_in.1, s32[64,128]{1,0:T(8,128)} %pad.8.meta_in, s32[8,128]{1,0:T(8,128)} %pad.9.em_in, bf16[2,64,256]{2,1,0:T(8,128)(2,1)} %bitcast.5, bf16[2048,8192]{1,0:T(8,128)(2,1)} %w_in.1), custom_call_target="tpu_custom_call" | custom-call | tf_op jit(solution)/shard_map/decode_step/pallas_call | solution.py:373
  80.4 1.7 %copy.21 = bf16[64,2048]{1,0:T(8,128)(2,1)} copy(bf16[64,2048]{1,0:T(8,128)(2,1)} %decode_step.1) | data formatting | bytes 524288
  (2 shorter events, 0.1 us)
Async XLA Ops:
  0.0 2.8 %copy-start = (bf16[64,2,1024]{2,1,0:T(2,128)(2,1)S(1)}, bf16[64,2,1024]{2,1,0:T(2,128)(2,1)}, u32[]{:S(2)}) copy-start(bf16[64,2,1024]{2,1,0:T(2,128)(2,1)} %param.8) | copy-start | bytes 786436

commit v4 on v3

--- a/solution.py
+++ b/solution.py
@@ -173,21 +173,10 @@
         for copy in copies:
             copy.start()
 
-    @pl.when(my_tp % 2 == 0)
-    def _():
-        start_all(page_copies(0, slice(None)))
-        start_all(query_copies(0))
-
-    @pl.when(my_tp % 2 == 1)
-    def _():
-        start_all(query_copies(0))
-        start_all(page_copies(0, slice(None)))
-
     for k in range(kv_heads):
+        start_all(query_copies(k))
+        start_all(page_copies(k, slice(None)))
         start_all(own_copies(k))
-        if k > 0:
-            start_all(page_copies(k, pl.ds(0, 1)))
-            start_all(query_copies(k))
 
     targets = tp_targets + [my_tp]
     w_copies = []
@@ -260,12 +249,6 @@
 
         def some(step, carry):
             head0 = k * per_kv + step * unroll
-            if k + 1 < kv_heads:
-
-                @pl.when(step < per_owner - 1)
-                def _():
-                    start_all(page_copies(k + 1, pl.ds(step + 1, 1)))
-
 
             def rows_of(block, inner):
                 for u in range(unroll):
@@ -285,9 +268,6 @@
             return carry
 
         lax.fori_loop(0, steps, some, 0)
-        for p in range(steps + 1, per_owner):
-            if k + 1 < kv_heads:
-                start_all(page_copies(k + 1, pl.ds(p, 1)))
         start_all(stat_copies(k))
 
     block = min(512, share)

time: 82.3 us -> 82.2 us (level)
  no operation moved by 1% of the time
where the time goes in v4:
time: 82.2 us; the launch traced here: 82 us
  Pallas kernels  76.8 us (93%)
  local copies, waits for them, and re-layouts  3.66 us (4%)
  other arithmetic  1.52 us (2%)
    pallas_call x1, Pallas kernels, per_device(): pl.pallas_call(functools.partial(step_kernel, list_len), out_shape=jax.Sh...  76.8 us
    unnamed x4, local copies, waits for them, and re-layouts  2.31 us

profile of v4, /device:TPU:1, one launch (start us, length us, event | category | flops | bytes accessed | tf_op | source)
XLA Modules:
  0.0 82.0 jit_solution(965161875560434601)
XLA Ops:
  0.0 0.0 copy-start
  0.0 0.8 select_reduce_fusion
  0.8 0.6 pad.9.em_in
  1.4 0.7 pad_add_fusion
  2.1 0.1 copy.15
  2.2 0.6 pad.8.meta_in
  2.8 0.0 copy-done
  2.9 0.6 copy.19
  3.5 76.8 %decode_step.1 = bf16[64,2048]{1,0:T(8,128)(2,1)} custom-call(bf16[64,2048]{1,0:T(8,128)(2,1)} %q_in.1, bf16[4,2,128,1024]{3,2,1,0:T(8,128)(2,1)} %kv_in.1, s32[64,128]{1,0:T(8,128)} %pad.8.meta_in, s32[8,128]{1,0:T(8,128)} %pad.9.em_in, bf16[2,64,256]{2,1,0:T(8,128)(2,1)} %bitcast.5, bf16[2048,8192]{1,0:T(8,128)(2,1)} %w_in.1), custom_call_target="tpu_custom_call" | custom-call | tf_op jit(solution)/shard_map/decode_step/pallas_call | solution.py:353
  80.3 1.7 %copy.21 = bf16[64,2048]{1,0:T(8,128)(2,1)} copy(bf16[64,2048]{1,0:T(8,128)(2,1)} %decode_step.1) | data formatting | bytes 524288
  (2 shorter events, 0.1 us)
Async XLA Ops:
  0.0 2.8 %copy-start = (bf16[64,2,1024]{2,1,0:T(2,128)(2,1)S(1)}, bf16[64,2,1024]{2,1,0:T(2,128)(2,1)}, u32[]{:S(2)}) copy-start(bf16[64,2,1024]{2,1,0:T(2,128)(2,1)} %param.8) | copy-start | bytes 786436
